TPU v7x, 32 devices: a whole 2x2x4 slice. The times are simulated.
32 devices in a mesh: rows: 8 (over y, x, core), cols: 4 (over z).
Axes of the slice: x: 2, y: 2, z: 4, core: 2. Of those that a mesh axis runs over, the one named last changes fastest.
Arguments:
- matrix: float32 [16384, 512], P('rows', 'cols'), may hold values from -48 to 48
- partners: int32 [2, 4], replicated, may hold values from 0 to 3, each once within a row
Outputs:
- rotated: float32 [16384, 512], P('rows', 'cols')
Inputs may be any that keep to these rules, and one draw needn't show every extreme that they name: Each row of partners names every block once.
All inputs are finite; a program needn't handle non-finite values.
Results may differ from a plain program's by a relative error of at most 0.00028.
Values sent between devices are 32-bit elements; how exact they have to be, the bound alone decides.
No kernel may reach another device: no remote copies, remote signals or barrier semaphores. Data moves between devices by JAX's collectives and lax.ppermute only.
A program may use at most 64 MiB of HBM per device.

v0:
```python
import jax
import jax.numpy as jnp
from jax import lax
from jax.sharding import PartitionSpec as P

CYCLE = 3
MATCHED = 2
STEPS = 12
epsilon = 1e-06
highest = lax.Precision.HIGHEST


def from_behind(array, axis, by):
    count = lax.axis_size(axis)
    return lax.ppermute(array, axis, [(i, (i + by) % count) for i in range(count)])


def start_iterate(gram_full):
    order = gram_full.shape[0]
    scale = lax.rsqrt(jnp.diagonal(gram_full) + epsilon)
    normed = gram_full * scale[:, None] * scale[None, :]
    kernel = jnp.eye(order, dtype=jnp.float32) + jnp.triu(normed, 1) - jnp.tril(normed, -1)
    return kernel / jnp.sqrt(jnp.sum(kernel * kernel))


def polar_whole(start):

    def advance(counter, current):
        inner = jnp.dot(current.T, current, precision=highest)
        return 1.5 * current - 0.5 * jnp.dot(current, inner, precision=highest)

    return lax.fori_loop(0, STEPS, advance, start)


def body(matrix, partners):
    current = matrix
    row_count, width = current.shape
    groups = lax.axis_size("cols")
    for meeting in range(CYCLE + MATCHED):
        if meeting < CYCLE:
            other = from_behind(current, "cols", meeting + 1)
        else:
            pieces = current.reshape(groups, row_count // groups, width)
            spread = lax.all_to_all(pieces, "cols", split_axis=0, concat_axis=0, tiled=True)
            chosen = jnp.take(spread, partners[meeting - CYCLE], axis=0)
            other = lax.all_to_all(chosen, "cols", split_axis=0, concat_axis=0, tiled=True).reshape(
                row_count, width
            )
        paired = jnp.concatenate([other, current], axis=1)
        local_gram = jnp.einsum("ra,rb->ab", paired, paired, precision=highest)
        gram_sum = lax.psum(local_gram, "rows")
        start = start_iterate(gram_sum)
        rotation = polar_whole(start)
        current = jnp.dot(paired, rotation[:, width:], precision=highest)
    return current


def solution(mesh):
    placed = (P("rows", "cols"), P())
    return jax.shard_map(
        body, mesh=mesh, in_specs=placed, out_specs=P("rows", "cols"), check_vma=False
    )
```

profile of v0, /device:TPU:0, one launch (start us, length us, event | category | flops | bytes accessed | tf_op | source)
XLA Modules:
  0.0 627.4 jit_solution(489708078406153949)
XLA Ops:
  6.5 3.1 collective-permute-start
  9.6 25.5 %collective-permute-done = f32[2048,128]{1,0:T(8,128)S(1)} collective-permute-done((f32[2048,128]{1,0:T(8,128)}, f32[2048,128]{1,0:T(8,128)S(1)}, u32[]{:S(2)}, u32[]{:S(2)}) %collective-permute-start) | collective-permute-done | bytes 1048608 | tf_op jit(solution)/shard_map/ppermute | solution.py:15
  35.2 4.3 fusion.42
  39.7 53.3 %all-reduce.6.cloned.1.call-done = f32[256,256]{1,0:T(8,128)} async-done(((f32[256,256]{1,0:T(8,128)}), f32[256,256]{1,0:T(8,128)}) %all-reduce.6.cloned.1.call-update) | async-done | bytes 262160 | tf_op jit(solution)/shard_map/psum | solution.py:51
  92.9 2.6 gather_fusion
  95.5 1.7 multiply_reduce_fusion.4
  97.9 1.1 broadcast_divide_fusion.4
  99.2 12.7 %while.50 = (s32[]{:T(128)}, f32[256,256]{0,1:T(8,128)S(1)}, s32[]{:T(128)}) while((s32[]{:T(128)}, f32[256,256]{0,1:T(8,128)S(1)}, s32[]{:T(128)}) %tuple.85), condition=%wide.region_3.4_spmd, body=%wide.region_2.3_spmd.sunk | while | flops 402849792 | bytes 1835053 | solution.py:32
  99.6 0.6 fusion.101
  100.7 0.6 fusion.101
  111.9 2.3 fusion.27
  114.2 2.5 collective-permute-start.1
  116.7 45.1 %collective-permute-done.1 = f32[2048,128]{0,1:T(8,128)S(1)} collective-permute-done((f32[2048,128]{0,1:T(8,128)S(1)}, f32[2048,128]{0,1:T(8,128)S(1)}, u32[]{:S(2)}, u32[]{:S(2)}) %collective-permute-start.1) | collective-permute-done | bytes 1048608 | tf_op jit(solution)/shard_map/ppermute | solution.py:15
  161.8 2.6 fusion.17
  164.9 52.8 %all-reduce.8.cloned.1.call-done = f32[256,256]{1,0:T(8,128)} async-done(((f32[256,256]{1,0:T(8,128)}), f32[256,256]{1,0:T(8,128)}) %all-reduce.8.cloned.1.call-update) | async-done | bytes 262160 | tf_op jit(solution)/shard_map/psum | solution.py:51
  217.7 2.6 gather_fusion.1
  220.3 1.7 multiply_reduce_fusion.3
  222.7 1.1 broadcast_divide_fusion.3
  224.0 12.8 %while.51 = (s32[]{:T(128)}, f32[256,256]{0,1:T(8,128)S(1)}, s32[]{:T(128)}) while((s32[]{:T(128)}, f32[256,256]{0,1:T(8,128)S(1)}, s32[]{:T(128)}) %tuple.88), condition=%wide.region_7.8_spmd, body=%wide.region_6.7_spmd.sunk | while | flops 402849792 | bytes 1835053 | solution.py:32
  226.5 0.6 fusion.107
  227.6 0.6 fusion.107
  230.8 0.6 fusion.107
  231.9 0.6 fusion.107
  232.9 0.6 fusion.107
  236.1 0.6 fusion.107
  236.7 1.3 fusion.16
  238.0 3.4 collective-permute-start.2
  241.4 21.6 %collective-permute-done.2 = f32[2048,128]{0,1:T(8,128)S(1)} collective-permute-done((f32[2048,128]{0,1:T(8,128)S(1)}, f32[2048,128]{0,1:T(8,128)S(1)}, u32[]{:S(2)}, u32[]{:S(2)}) %collective-permute-start.2) | collective-permute-done | bytes 1048608 | tf_op jit(solution)/shard_map/ppermute | solution.py:15
  263.0 2.6 fusion.15
  265.6 54.3 %all-reduce.10.cloned.1.call-done = f32[256,256]{1,0:T(8,128)} async-done(((f32[256,256]{1,0:T(8,128)}), f32[256,256]{1,0:T(8,128)}) %all-reduce.10.cloned.1.call-update) | async-done | bytes 262160 | tf_op jit(solution)/shard_map/psum | solution.py:51
  319.9 2.6 gather_fusion.2
  322.5 1.7 multiply_reduce_fusion.2
  325.0 1.1 broadcast_divide_fusion.2
  326.2 12.7 %while.52 = (s32[]{:T(128)}, f32[256,256]{0,1:T(8,128)S(1)}, s32[]{:T(128)}) while((s32[]{:T(128)}, f32[256,256]{0,1:T(8,128)S(1)}, s32[]{:T(128)}) %tuple.91), condition=%wide.region_11.12_spmd, body=%wide.region_10.11_spmd.sunk | while | flops 402849792 | bytes 1835053 | solution.py:32
  326.6 0.6 fusion.113
  327.7 0.6 fusion.113
  338.9 4.5 fusion.14
  343.5 4.6 all-to-all-start
  348.1 24.9 %all-to-all-done = f32[4,512,128]{2,1,0:T(8,128)S(1)} async-done(((f32[4,512,128]{2,1,0:T(8,128)}), f32[4,512,128]{2,1,0:T(8,128)S(1)}, u32[]{:S(2)}, u32[]{:S(2)}) %all-to-all-start) | async-done | bytes 1048608 | tf_op jit(solution)/shard_map/all_to_all | solution.py:44
  373.0 0.6 gather_fusion.5
  373.8 27.9 %all_to_all.20 = f32[4,512,128]{2,1,0:T(8,128)S(1)} all-to-all(f32[4,512,128]{2,1,0:T(8,128)S(1)} %broadcast_select_fusion.1), channel_id=1, replica_groups=mesh['rows'=8,'cols'=4] {'cols'}, dimensions={0} | all-to-all | bytes 2097152 | tf_op jit(solution)/shard_map/all_to_all | solution.py:46
  401.7 5.9 fusion.13
  407.6 51.5 %all-reduce.12.cloned.1.call-done = f32[256,256]{1,0:T(8,128)} async-done(((f32[256,256]{1,0:T(8,128)}), f32[256,256]{1,0:T(8,128)}) %all-reduce.12.cloned.1.call-update) | async-done | bytes 262160 | tf_op jit(solution)/shard_map/psum | solution.py:51
  459.1 2.6 gather_fusion.3
  461.6 1.8 multiply_reduce_fusion.1
  464.1 1.1 broadcast_divide_fusion.1
  465.3 12.7 %while.53 = (s32[]{:T(128)}, f32[256,256]{0,1:T(8,128)S(1)}, s32[]{:T(128)}) while((s32[]{:T(128)}, f32[256,256]{0,1:T(8,128)S(1)}, s32[]{:T(128)}) %tuple.94), condition=%wide.region_15.17_spmd, body=%wide.region_14.16_spmd.sunk | while | flops 402849792 | bytes 1835053 | solution.py:32
  465.8 0.6 fusion.119
  478.1 4.0 fusion.12
  482.1 4.6 all-to-all-start.2
  486.7 24.9 %all-to-all-done.2 = f32[4,512,128]{2,1,0:T(8,128)S(1)} async-done(((f32[4,512,128]{2,1,0:T(8,128)}), f32[4,512,128]{2,1,0:T(8,128)S(1)}, u32[]{:S(2)}, u32[]{:S(2)}) %all-to-all-start.2) | async-done | bytes 1048608 | tf_op jit(solution)/shard_map/all_to_all | solution.py:44
  511.6 0.6 gather_fusion.6
  512.4 27.9 %all_to_all.21 = f32[4,512,128]{2,1,0:T(8,128)S(1)} all-to-all(f32[4,512,128]{2,1,0:T(8,128)S(1)} %broadcast_select_fusion), channel_id=1, replica_groups=mesh['rows'=8,'cols'=4] {'cols'}, dimensions={0} | all-to-all | bytes 2097152 | tf_op jit(solution)/shard_map/all_to_all | solution.py:46
  540.3 5.9 fusion.11
  546.2 51.5 %all-reduce.14.cloned.1.call-done = f32[256,256]{1,0:T(8,128)} async-done(((f32[256,256]{1,0:T(8,128)}), f32[256,256]{1,0:T(8,128)}) %all-reduce.14.cloned.1.call-update) | async-done | bytes 262160 | tf_op jit(solution)/shard_map/psum | solution.py:51
  597.7 2.6 gather_fusion.4
  600.3 1.7 multiply_reduce_fusion
  602.7 1.1 broadcast_divide_fusion
  603.9 12.8 %while.54 = (s32[]{:T(128)}, f32[256,256]{0,1:T(8,128)S(1)}, s32[]{:T(128)}) while((s32[]{:T(128)}, f32[256,256]{0,1:T(8,128)S(1)}, s32[]{:T(128)}) %tuple.97), condition=%wide.region_19.21_spmd, body=%wide.region_18.20_spmd.sunk | while | flops 402849792 | bytes 1835053 | solution.py:32
  605.4 0.6 fusion.125
  606.5 0.6 fusion.125
  611.8 0.6 fusion.125
  615.0 0.6 fusion.125
  616.7 4.0 fusion.10
  (198 shorter events, 54.2 us)
Async XLA Ops:
  6.5 28.6 %copy-start = (f32[2048,128]{1,0:T(8,128)S(1)}, f32[2048,128]{1,0:T(8,128)}, u32[]{:S(2)}) copy-start(f32[2048,128]{1,0:T(8,128)} %param.14) | copy-start | bytes 3145732
  6.5 86.4 %all-reduce.6.cloned.1.call-start = ((), (), s32[]{:S(2)}) async-start(), calls=%async_computation.4 | async-start | bytes 524288 | tf_op jit(solution)/shard_map/psum | solution.py:51
  6.5 28.5 %collective-permute-start = (f32[2048,128]{1,0:T(8,128)}, f32[2048,128]{1,0:T(8,128)S(1)}, u32[]{:S(2)}, u32[]{:S(2)}) collective-permute-start(f32[2048,128]{1,0:T(8,128)} %param.14), channel_id=1, source_target_pairs={{0,1},{1,2},{2,3},{3,0},{4,5},{5,6},{6,7},{7,4},{8,9},{9,10},{10,1... | collective-permute-start | bytes 3145736 | tf_op jit(solution)/shard_map/ppermute | solution.py:15
  39.6 178.1 %all-reduce.8.cloned.1.call-start = ((), (), s32[]{:S(2)}) async-start(), calls=%async_computation.5 | async-start | bytes 524288 | tf_op jit(solution)/shard_map/psum | solution.py:51
  114.2 47.6 %collective-permute-start.1 = (f32[2048,128]{0,1:T(8,128)S(1)}, f32[2048,128]{0,1:T(8,128)S(1)}, u32[]{:S(2)}, u32[]{:S(2)}) collective-permute-start(f32[2048,128]{0,1:T(8,128)S(1)} %fusion.27), channel_id=1, source_target_pairs={{0,2},{1,3},{2,0},{3,1},{4,6},{5,7},{6,4},{7,5},{8,10},{9,11},{10,... | collective-permute-start | bytes 3145736 | tf_op jit(solution)/shard_map/ppermute | solution.py:15
  164.4 155.6 %all-reduce.10.cloned.1.call-start = ((), (), s32[]{:S(2)}) async-start(), calls=%async_computation.6 | async-start | bytes 524288 | tf_op jit(solution)/shard_map/psum | solution.py:51
  238.0 25.0 %collective-permute-start.2 = (f32[2048,128]{0,1:T(8,128)S(1)}, f32[2048,128]{0,1:T(8,128)S(1)}, u32[]{:S(2)}, u32[]{:S(2)}) collective-permute-start(f32[2048,128]{0,1:T(8,128)S(1)} %fusion.16), channel_id=1, source_target_pairs={{0,3},{1,0},{2,1},{3,2},{4,7},{5,4},{6,5},{7,6},{8,11},{9,8},{10,9... | collective-permute-start | bytes 3145736 | tf_op jit(solution)/shard_map/ppermute | solution.py:15
  338.9 9.2 %copy-start.1 = (s32[2,4]{1,0:T(2,128)S(1)}, s32[2,4]{1,0:T(2,128)}, u32[]{:S(2)}) copy-start(s32[2,4]{1,0:T(2,128)} %param.15) | copy-start | bytes 100
  343.5 29.5 %all-to-all-start = ((f32[4,512,128]{2,1,0:T(8,128)}), f32[4,512,128]{2,1,0:T(8,128)S(1)}, u32[]{:S(2)}, u32[]{:S(2)}) async-start(f32[4,512,128]{2,1,0:T(8,128)} %bitcast.8), calls=%async_computation | async-start | bytes 2097152 | tf_op jit(solution)/shard_map/all_to_all | solution.py:44
  348.1 111.0 %all-reduce.12.cloned.1.call-start = ((), (), s32[]{:S(2)}) async-start(), calls=%async_computation.7 | async-start | bytes 524288 | tf_op jit(solution)/shard_map/psum | solution.py:51
  482.1 29.5 %all-to-all-start.2 = ((f32[4,512,128]{2,1,0:T(8,128)}), f32[4,512,128]{2,1,0:T(8,128)S(1)}, u32[]{:S(2)}, u32[]{:S(2)}) async-start(f32[4,512,128]{2,1,0:T(8,128)} %bitcast.10), calls=%async_computation.2 | async-start | bytes 2097152 | tf_op jit(solution)/shard_map/all_to_all | solution.py:44
  486.7 111.0 %all-reduce.14.cloned.1.call-start = ((), (), s32[]{:S(2)}) async-start(), calls=%async_computation.8 | async-start | bytes 524288 | tf_op jit(solution)/shard_map/psum | solution.py:51
Sparse Core Ops, SparseCore 0:
  39.7 53.1 all-reduce.5
  164.5 53.1 all-reduce.7
  265.7 54.1 all-reduce.9
  407.7 51.3 all-reduce.11
  546.3 51.3 all-reduce.13
where the time goes:
time: 636 us; the launch traced here: 627 us
  waiting for transfers between devices  405 us (64%)
  matrix products  97.6 us (15%)
  blocking collectives  55.8 us (9%)
  starting transfers between devices  18.7 us (3%)
  between operations  17 us (3%)
  local copies, waits for them, and re-layouts  16 us (3%)
  other arithmetic  14.5 us (2%)
    psum x5, waiting for transfers between devices, body(): gram_sum = lax.psum(local_gram, 'rows')  263 us
    ppermute x3, waiting for transfers between devices, from_behind(): lax.ppermute(array, axis, [(i, (i + by) % count) for i in range(count)])  92.1 us
    all_to_all x2, blocking collectives, body(): lax.all_to_all(chosen, 'cols', split_axis=0, concat_axis=0, tiled=True)  55.8 us
    all_to_all x2, waiting for transfers between devices, body(): lax.all_to_all(pieces, 'cols', split_axis=0, concat_axis=0, tiled=True)  49.8 us
    dot_general x60, matrix products, advance(): return 1.5 * current - 0.5 * jnp.dot(current, inner, precision=highest)  35.9 us
    dot_general x60, matrix products, advance(): inner = jnp.dot(current.T, current, precision=highest)  24.4 us
    dot_general x5, matrix products, body(): local_gram = jnp.einsum('ra,rb->ab', paired, paired, precision=highest)  21.2 us
    dot_general x5, matrix products, body(): current = jnp.dot(paired, rotation[:, width:], precision=highest)  16.2 us
  transfers between devices with their start and end apart: 10, of which 10 were waited for; matrix products, arithmetic and copies ran while one was open for 0% of the time, Pallas kernels for 0%

commit v1 on v0

--- a/solution.py
+++ b/solution.py
@@ -1,3 +1,4 @@
+import functools
 import jax
 import jax.numpy as jnp
 from jax import lax
@@ -8,6 +9,14 @@
 STEPS = 12
 epsilon = 1e-06
 highest = lax.Precision.HIGHEST
+
+
+def _push_quotas(load, chip_axis):
+    before = lax.all_gather(load, axis_name=chip_axis)
+    return jnp.sum(before, axis=0)
+
+
+axis_part_plan = functools.partial(_push_quotas, chip_axis="rows")
 
 
 def from_behind(array, axis, by):
@@ -48,7 +57,7 @@
             )
         paired = jnp.concatenate([other, current], axis=1)
         local_gram = jnp.einsum("ra,rb->ab", paired, paired, precision=highest)
-        gram_sum = lax.psum(local_gram, "rows")
+        gram_sum = axis_part_plan(local_gram)
         start = start_iterate(gram_sum)
         rotation = polar_whole(start)
         current = jnp.dot(paired, rotation[:, width:], precision=highest)

time: 636 us -> 512 us (0.81)
  waiting for transfers between devices: 405 us -> 282 us
    psum x5 -> x0, waiting for transfers between devices: 263 us -> none  [body(): gram_sum = lax.psum(local_gram, 'rows')]
    all_gather x0 -> x5, waiting for transfers between devices: none -> 136 us  [_push_quotas(): before = lax.all_gather(load, axis_name=chip_axis)]
    reduce_sum x0 -> x5, other arithmetic: none -> 8.8 us  [_push_quotas(): return jnp.sum(before, axis=0)]
where the time goes in v1:
time: 512 us; the launch traced here: 505 us
  waiting for transfers between devices  282 us (55%)
  matrix products  99 us (19%)
  blocking collectives  55.8 us (11%)
  starting transfers between devices  18.6 us (4%)
  between operations  17 us (3%)
  local copies, waits for them, and re-layouts  15.9 us (3%)
  other arithmetic  13.7 us (3%)
    all_gather x5, waiting for transfers between devices, _push_quotas(): before = lax.all_gather(load, axis_name=chip_axis)  136 us
    ppermute x3, waiting for transfers between devices, from_behind(): lax.ppermute(array, axis, [(i, (i + by) % count) for i in range(count)])  94.5 us
    all_to_all x2, blocking collectives, body(): lax.all_to_all(chosen, 'cols', split_axis=0, concat_axis=0, tiled=True)  55.8 us
    all_to_all x2, waiting for transfers between devices, body(): lax.all_to_all(pieces, 'cols', split_axis=0, concat_axis=0, tiled=True)  52.2 us
    dot_general x60, matrix products, advance(): return 1.5 * current - 0.5 * jnp.dot(current, inner, precision=highest)  35.9 us
    dot_general x60, matrix products, advance(): inner = jnp.dot(current.T, current, precision=highest)  24.4 us
    dot_general x5, matrix products, body(): local_gram = jnp.einsum('ra,rb->ab', paired, paired, precision=highest)  21.3 us
    dot_general x5, matrix products, body(): current = jnp.dot(paired, rotation[:, width:], precision=highest)  17.4 us
  transfers between devices with their start and end apart: 10, of which 10 were waited for; matrix products, arithmetic and copies ran while one was open for 0% of the time, Pallas kernels for 0%

profile of v1, /device:TPU:0, one launch (start us, length us, event | category | flops | bytes accessed | tf_op | source)
XLA Modules:
  0.0 504.6 jit_solution(9530485871418048939)
XLA Ops:
  6.5 3.1 collective-permute-start
  9.6 25.5 %collective-permute-done = f32[2048,128]{1,0:T(8,128)S(1)} collective-permute-done((f32[2048,128]{1,0:T(8,128)}, f32[2048,128]{1,0:T(8,128)S(1)}, u32[]{:S(2)}, u32[]{:S(2)}) %collective-permute-start) | collective-permute-done | bytes 1048608 | tf_op jit(solution)/shard_map/ppermute | solution.py:24
  35.2 4.3 fusion.42
  39.7 27.2 %all-gather.11.cloned.1.call-done = f32[2048,256]{1,0:T(8,128)} async-done(((f32[256,256]{1,0:T(8,128)}), f32[2048,256]{1,0:T(8,128)}) %all-gather.11.cloned.1.call-update) | async-done | bytes 2097168 | tf_op jit(solution)/shard_map/all_gather | solution.py:15
  66.8 1.8 reduce_sum.90
  68.6 2.3 gather_fusion
  71.0 0.8 multiply_reduce_fusion.4
  72.7 12.7 %while.50 = (s32[]{:T(128)}, f32[256,256]{0,1:T(8,128)S(1)}, s32[]{:T(128)}) while((s32[]{:T(128)}, f32[256,256]{0,1:T(8,128)S(1)}, s32[]{:T(128)}) %tuple.85), condition=%wide.region_3.4_spmd, body=%wide.region_2.3_spmd.sunk | while | flops 402849792 | bytes 1835053 | solution.py:41
  85.5 2.3 fusion.27
  87.8 2.5 collective-permute-start.1
  90.2 46.3 %collective-permute-done.1 = f32[2048,128]{0,1:T(8,128)S(1)} collective-permute-done((f32[2048,128]{0,1:T(8,128)S(1)}, f32[2048,128]{0,1:T(8,128)S(1)}, u32[]{:S(2)}, u32[]{:S(2)}) %collective-permute-start.1) | collective-permute-done | bytes 1048608 | tf_op jit(solution)/shard_map/ppermute | solution.py:24
  136.5 1.0 copy-done
  137.5 2.6 fusion.17
  140.6 27.4 %all-gather.13.cloned.1.call-done = f32[2048,256]{1,0:T(8,128)} async-done(((f32[256,256]{1,0:T(8,128)}), f32[2048,256]{1,0:T(8,128)}) %all-gather.13.cloned.1.call-update) | async-done | bytes 2097168 | tf_op jit(solution)/shard_map/all_gather | solution.py:15
  168.0 1.8 reduce_sum.92
  169.8 2.3 gather_fusion.1
  172.1 0.8 multiply_reduce_fusion.3
  173.8 12.7 %while.51 = (s32[]{:T(128)}, f32[256,256]{0,1:T(8,128)S(1)}, s32[]{:T(128)}) while((s32[]{:T(128)}, f32[256,256]{0,1:T(8,128)S(1)}, s32[]{:T(128)}) %tuple.88), condition=%wide.region_7.8_spmd, body=%wide.region_6.7_spmd.sunk | while | flops 402849792 | bytes 1835053 | solution.py:41
  186.5 2.5 fusion.16
  189.1 3.4 collective-permute-start.2
  192.5 22.8 %collective-permute-done.2 = f32[2048,128]{0,1:T(8,128)S(1)} collective-permute-done((f32[2048,128]{0,1:T(8,128)S(1)}, f32[2048,128]{0,1:T(8,128)S(1)}, u32[]{:S(2)}, u32[]{:S(2)}) %collective-permute-start.2) | collective-permute-done | bytes 1048608 | tf_op jit(solution)/shard_map/ppermute | solution.py:24
  215.3 2.6 fusion.15
  217.9 28.9 %all-gather.15.cloned.1.call-done = f32[2048,256]{1,0:T(8,128)} async-done(((f32[256,256]{1,0:T(8,128)}), f32[2048,256]{1,0:T(8,128)}) %all-gather.15.cloned.1.call-update) | async-done | bytes 2097168 | tf_op jit(solution)/shard_map/all_gather | solution.py:15
  246.7 1.8 reduce_sum.94
  248.5 2.3 gather_fusion.2
  250.9 0.8 multiply_reduce_fusion.2
  252.6 12.8 %while.52 = (s32[]{:T(128)}, f32[256,256]{0,1:T(8,128)S(1)}, s32[]{:T(128)}) while((s32[]{:T(128)}, f32[256,256]{0,1:T(8,128)S(1)}, s32[]{:T(128)}) %tuple.91), condition=%wide.region_11.12_spmd, body=%wide.region_10.11_spmd.sunk | while | flops 402849792 | bytes 1835053 | solution.py:41
  253.1 0.6 fusion.113
  254.1 0.6 fusion.113
  257.3 0.6 fusion.113
  258.4 0.6 fusion.113
  259.4 0.6 fusion.113
  262.6 0.6 fusion.113
  263.7 0.6 fusion.113
  264.8 0.6 fusion.113
  265.4 4.5 fusion.14
  269.9 4.6 all-to-all-start
  274.5 26.1 %all-to-all-done = f32[4,512,128]{2,1,0:T(8,128)S(1)} async-done(((f32[4,512,128]{2,1,0:T(8,128)}), f32[4,512,128]{2,1,0:T(8,128)S(1)}, u32[]{:S(2)}, u32[]{:S(2)}) %all-to-all-start) | async-done | bytes 1048608 | tf_op jit(solution)/shard_map/all_to_all | solution.py:53
  300.7 0.6 gather_fusion.5
  301.4 27.9 %all_to_all.20 = f32[4,512,128]{2,1,0:T(8,128)S(1)} all-to-all(f32[4,512,128]{2,1,0:T(8,128)S(1)} %broadcast_select_fusion.1), channel_id=1, replica_groups=mesh['rows'=8,'cols'=4] {'cols'}, dimensions={0} | all-to-all | bytes 2097152 | tf_op jit(solution)/shard_map/all_to_all | solution.py:55
  329.3 5.9 %fusion.13 = f32[256,256]{1,0:T(8,128)} fusion(f32[2048,128]{1,0:T(8,128)} %fusion.14, f32[2048,128]{1,0:T(8,128)S(1)} %bitcast.116), kind=kOutput, calls=%fused_computation.29 | convolution fusion | flops 1611137024 | bytes 2359296 | tf_op jit(solution)/shard_map/ra,rb->ab/dot_general | solution.py:59
  335.3 26.0 %all-gather.17.cloned.1.call-done = f32[2048,256]{1,0:T(8,128)} async-done(((f32[256,256]{1,0:T(8,128)}), f32[2048,256]{1,0:T(8,128)}) %all-gather.17.cloned.1.call-update) | async-done | bytes 2097168 | tf_op jit(solution)/shard_map/all_gather | solution.py:15
  361.3 1.8 reduce_sum.96
  363.0 2.3 gather_fusion.3
  365.4 0.8 multiply_reduce_fusion.1
  367.1 12.8 %while.53 = (s32[]{:T(128)}, f32[256,256]{0,1:T(8,128)S(1)}, s32[]{:T(128)}) while((s32[]{:T(128)}, f32[256,256]{0,1:T(8,128)S(1)}, s32[]{:T(128)}) %tuple.94), condition=%wide.region_15.17_spmd, body=%wide.region_14.16_spmd.sunk | while | flops 402849792 | bytes 1835053 | solution.py:41
  368.6 0.6 fusion.119
  371.8 0.6 fusion.119
  372.8 0.6 fusion.119
  373.9 0.6 fusion.119
  379.8 4.0 fusion.12
  383.8 4.6 all-to-all-start.2
  388.5 26.1 %all-to-all-done.2 = f32[4,512,128]{2,1,0:T(8,128)S(1)} async-done(((f32[4,512,128]{2,1,0:T(8,128)}), f32[4,512,128]{2,1,0:T(8,128)S(1)}, u32[]{:S(2)}, u32[]{:S(2)}) %all-to-all-start.2) | async-done | bytes 1048608 | tf_op jit(solution)/shard_map/all_to_all | solution.py:53
  414.6 0.6 gather_fusion.6
  415.3 27.9 %all_to_all.21 = f32[4,512,128]{2,1,0:T(8,128)S(1)} all-to-all(f32[4,512,128]{2,1,0:T(8,128)S(1)} %broadcast_select_fusion), channel_id=1, replica_groups=mesh['rows'=8,'cols'=4] {'cols'}, dimensions={0} | all-to-all | bytes 2097152 | tf_op jit(solution)/shard_map/all_to_all | solution.py:55
  443.3 5.9 %fusion.11 = f32[256,256]{1,0:T(8,128)} fusion(f32[2048,128]{1,0:T(8,128)} %fusion.12, f32[2048,128]{1,0:T(8,128)S(1)} %bitcast.114), kind=kOutput, calls=%fused_computation.27 | convolution fusion | flops 1611137024 | bytes 2359296 | tf_op jit(solution)/shard_map/ra,rb->ab/dot_general | solution.py:59
  449.2 26.1 %all-gather.19.cloned.1.call-done = f32[2048,256]{1,0:T(8,128)} async-done(((f32[256,256]{1,0:T(8,128)}), f32[2048,256]{1,0:T(8,128)}) %all-gather.19.cloned.1.call-update) | async-done | bytes 2097168 | tf_op jit(solution)/shard_map/all_gather | solution.py:15
  475.2 1.8 reduce_sum.98
  477.0 2.3 gather_fusion.4
  479.4 0.8 multiply_reduce_fusion
  481.1 12.8 %while.54 = (s32[]{:T(128)}, f32[256,256]{0,1:T(8,128)S(1)}, s32[]{:T(128)}) while((s32[]{:T(128)}, f32[256,256]{0,1:T(8,128)S(1)}, s32[]{:T(128)}) %tuple.97), condition=%wide.region_19.21_spmd, body=%wide.region_18.20_spmd.sunk | while | flops 402849792 | bytes 1835053 | solution.py:41
  483.7 0.6 fusion.125
  490.1 0.6 fusion.125
  493.9 4.0 fusion.10
  (205 shorter events, 55.5 us)
Async XLA Ops:
  6.5 28.6 %copy-start.1 = (f32[2048,128]{1,0:T(8,128)S(1)}, f32[2048,128]{1,0:T(8,128)}, u32[]{:S(2)}) copy-start(f32[2048,128]{1,0:T(8,128)} %param.14) | copy-start | bytes 3145732
  6.5 60.3 %all-gather.11.cloned.1.call-start = ((), (), s32[]{:S(2)}) async-start(), calls=%async_computation.4 | async-start | bytes 2359296 | tf_op jit(solution)/shard_map/all_gather | solution.py:15
  6.5 28.5 %collective-permute-start = (f32[2048,128]{1,0:T(8,128)}, f32[2048,128]{1,0:T(8,128)S(1)}, u32[]{:S(2)}, u32[]{:S(2)}) collective-permute-start(f32[2048,128]{1,0:T(8,128)} %param.14), channel_id=1, source_target_pairs={{0,1},{1,2},{2,3},{3,0},{4,5},{5,6},{6,7},{7,4},{8,9},{9,10},{10,1... | collective-permute-start | bytes 3145736 | tf_op jit(solution)/shard_map/ppermute | solution.py:24
  39.6 128.4 %all-gather.13.cloned.1.call-start = ((), (), s32[]{:S(2)}) async-start(), calls=%async_computation.5 | async-start | bytes 2359296 | tf_op jit(solution)/shard_map/all_gather | solution.py:15
  87.8 48.7 %collective-permute-start.1 = (f32[2048,128]{0,1:T(8,128)S(1)}, f32[2048,128]{0,1:T(8,128)S(1)}, u32[]{:S(2)}, u32[]{:S(2)}) collective-permute-start(f32[2048,128]{0,1:T(8,128)S(1)} %fusion.27), channel_id=1, source_target_pairs={{0,2},{1,3},{2,0},{3,1},{4,6},{5,7},{6,4},{7,5},{8,10},{9,11},{10,... | collective-permute-start | bytes 3145736 | tf_op jit(solution)/shard_map/ppermute | solution.py:24
  136.5 1.0 copy-start
  140.1 106.6 %all-gather.15.cloned.1.call-start = ((), (), s32[]{:S(2)}) async-start(), calls=%async_computation.6 | async-start | bytes 2359296 | tf_op jit(solution)/shard_map/all_gather | solution.py:15
  189.1 26.2 %collective-permute-start.2 = (f32[2048,128]{0,1:T(8,128)S(1)}, f32[2048,128]{0,1:T(8,128)S(1)}, u32[]{:S(2)}, u32[]{:S(2)}) collective-permute-start(f32[2048,128]{0,1:T(8,128)S(1)} %fusion.16), channel_id=1, source_target_pairs={{0,3},{1,0},{2,1},{3,2},{4,7},{5,4},{6,5},{7,6},{8,11},{9,8},{10,9... | collective-permute-start | bytes 3145736 | tf_op jit(solution)/shard_map/ppermute | solution.py:24
  265.4 9.1 %copy-start.2 = (s32[2,4]{1,0:T(2,128)S(1)}, s32[2,4]{1,0:T(2,128)}, u32[]{:S(2)}) copy-start(s32[2,4]{1,0:T(2,128)} %param.15) | copy-start | bytes 100
  269.9 30.7 %all-to-all-start = ((f32[4,512,128]{2,1,0:T(8,128)}), f32[4,512,128]{2,1,0:T(8,128)S(1)}, u32[]{:S(2)}, u32[]{:S(2)}) async-start(f32[4,512,128]{2,1,0:T(8,128)} %bitcast.11), calls=%async_computation | async-start | bytes 2097152 | tf_op jit(solution)/shard_map/all_to_all | solution.py:53
  274.5 86.8 %all-gather.17.cloned.1.call-start = ((), (), s32[]{:S(2)}) async-start(), calls=%async_computation.7 | async-start | bytes 2359296 | tf_op jit(solution)/shard_map/all_gather | solution.py:15
  383.8 30.7 %all-to-all-start.2 = ((f32[4,512,128]{2,1,0:T(8,128)}), f32[4,512,128]{2,1,0:T(8,128)S(1)}, u32[]{:S(2)}, u32[]{:S(2)}) async-start(f32[4,512,128]{2,1,0:T(8,128)} %bitcast.14), calls=%async_computation.2 | async-start | bytes 2097152 | tf_op jit(solution)/shard_map/all_to_all | solution.py:53
  388.4 86.8 %all-gather.19.cloned.1.call-start = ((), (), s32[]{:S(2)}) async-start(), calls=%async_computation.8 | async-start | bytes 2359296 | tf_op jit(solution)/shard_map/all_gather | solution.py:15
Sparse Core Ops, SparseCore 0:
  39.7 27.0 all-gather.10
  140.2 27.7 all-gather.12
  218.0 28.7 all-gather.14
  335.4 25.8 all-gather.16
  449.3 25.8 all-gather.18
